TPU v7x, 32 devices: a whole 2x2x4 slice. The times are simulated.
32 devices in a mesh: row: 8 (over y, x, core), col: 4 (over z).
Axes of the slice: x: 2, y: 2, z: 4, core: 2. Of those that a mesh axis runs over, the one named last changes fastest.
Arguments:
- panel_u: bfloat16 [2, 8, 1024, 160], P(None, 'row', 'col'), may hold values from -6 to 6
- panel_v: bfloat16 [2, 8, 1024, 160], P(None, 'row', 'col'), may hold values from -0.0625 to 0.0625
- panel_rank: int32 [2, 8], P(None, 'row'), may hold values from 32 to 160, as said below
- diag_inverse: bfloat16 [1024, 1024], P('col'), as said below
- tile_u: bfloat16 [2, 8, 4, 1024, 160], P(None, 'row', 'col'), may hold values from -6 to 6
- tile_v: bfloat16 [2, 8, 4, 1024, 160], P(None, 'row', 'col'), may hold values from -0.5 to 0.5
- tile_rank: int32 [2, 8, 4], P(None, 'row', 'col'), may hold values from 32 to 160, as said below
- sketch: bfloat16 [2, 8, 4, 1024, 160], P(None, 'row', 'col'), may hold values from -6 to 6
Outputs:
- new_u: float32 [2, 8, 4, 1024, 160], P(None, 'row', 'col')
- new_v: float32 [2, 8, 4, 1024, 160], P(None, 'row', 'col')
Inputs may be any that keep to these rules, and one draw needn't show every extreme that they name: `panel_rank`: some panel tile has rank 160. `tile_rank`: some trailing tile has rank 160. `diag_inverse`: lower triangular with diagonal entries of 1 to 2.
All inputs are finite; a program needn't handle non-finite values.
Results may differ from a plain program's by a relative error of at most 0.0037.
Values may be sent and summed in bfloat16 or wider, within the bound.
No kernel may reach another device: no remote copies, remote signals or barrier semaphores. Data moves between devices by JAX's collectives and lax.ppermute only.
A program may use at most 64 MiB of HBM per device.

v0:
```python
import math
import jax
import jax.numpy as jnp
from jax import lax
from jax.sharding import PartitionSpec as P


def spread(value, axis, source):
    kept = jnp.where(lax.axis_index(axis) == source, value, 0).astype(value.dtype)
    return lax.psum(kept, axis)


def recompress(old_u, old_v, row_u, row_s, col_u, col_s, omega, rank):
    high = lax.Precision.HIGHEST
    width = old_u.shape[1]
    keep_flag = jnp.arange(width, dtype=jnp.int32) < rank
    keep = keep_flag.astype(jnp.float32)
    keep_half = keep_flag.astype(jnp.bfloat16)
    ou_half = old_u * keep_half
    ov_half = old_v * keep_half
    om_half = omega * keep_half
    coupling = jnp.dot(row_s.T, col_s, preferred_element_type=jnp.float32)
    small_left = jnp.dot(ov_half.T, om_half, preferred_element_type=jnp.float32)
    small_right = jnp.dot(col_u.T, om_half, preferred_element_type=jnp.float32)
    ou = ou_half.astype(jnp.float32)
    ov = ov_half.astype(jnp.float32)
    ru = row_u.astype(jnp.float32)
    cu = col_u.astype(jnp.float32)
    sketched = jnp.dot(ou, small_left, precision=high)
    sketched = sketched - jnp.dot(
        ru, jnp.dot(coupling, small_right, precision=high), precision=high
    )
    gram = jnp.dot(sketched.T, sketched, precision=high) + jnp.diag(1.0 - keep)
    lower = jnp.linalg.cholesky(gram)
    basis = lax.linalg.triangular_solve(
        lower, sketched, left_side=False, lower=True, transpose_a=True
    )
    factor = math.sqrt(old_u.shape[0])
    right = jnp.dot(ov, jnp.dot(ou.T, basis, precision=high), precision=high)
    right = right - jnp.dot(
        cu,
        jnp.dot(coupling.T, jnp.dot(ru.T, basis, precision=high), precision=high),
        precision=high,
    )
    return (basis * factor, right / factor)


def on_device(panel_u, panel_v, panel_rank, diag_inverse, tile_u, tile_v, tile_rank, sketch):
    width = panel_u.shape[3]
    keep = (
        jnp.arange(width, dtype=jnp.int32)[None, None, None, :] < panel_rank[:, :, None, None]
    ).astype(jnp.bfloat16)
    full_u, full_v = (
        lax.all_gather(panel_u * keep, "col", axis=2, tiled=True),
        lax.all_gather(panel_v * keep, "col", axis=2, tiled=True),
    )
    inverse = lax.all_gather(diag_inverse, "col", axis=0, tiled=True)
    solved = jnp.einsum(
        "ab,tsbr->tsar", inverse, full_v, preferred_element_type=jnp.float32
    ).astype(jnp.bfloat16)
    col_count = lax.axis_size("col")
    col_place = lax.axis_index("col")
    results_u = []
    results_v = []
    for column in range(tile_u.shape[0]):
        source = column * col_count + col_place
        col_u, col_s = (spread(full_u[0, 0], "row", source), spread(solved[0, 0], "row", source))
        fresh_u, fresh_v = recompress(
            tile_u[column, 0, 0],
            tile_v[column, 0, 0],
            full_u[1, 0],
            solved[1, 0],
            col_u,
            col_s,
            sketch[column, 0, 0],
            tile_rank[column, 0, 0],
        )
        results_u.append(fresh_u)
        results_v.append(fresh_v)
    stacked_u = jnp.stack(results_u)[:, None, None]
    stacked_v = jnp.stack(results_v)[:, None, None]
    return (stacked_u, stacked_v)


def solution(mesh):
    placed = (
        P(None, "row", "col", None),
        P(None, "row", "col", None),
        P(None, "row"),
        P("col", None),
        P(None, "row", "col", None, None),
        P(None, "row", "col", None, None),
        P(None, "row", "col"),
        P(None, "row", "col", None, None),
    )
    return jax.shard_map(
        on_device,
        mesh=mesh,
        in_specs=placed,
        out_specs=(P(None, "row", "col", None, None), P(None, "row", "col", None, None)),
        check_vma=False,
    )
```

profile of v0, /device:TPU:0, one launch (start us, length us, event | category | flops | bytes accessed | tf_op | source)
XLA Modules:
  0.0 269.2 jit_solution(11368111475773620207)
XLA Ops:
  7.2 0.7 all-gather.2.cloned.1.call-update
  8.0 1.3 fusion.77
  9.3 0.6 fusion.71
  10.6 0.7 convert_subtract_fusion
  11.3 0.7 compare_convert_fusion
  12.0 1.1 bitcast_multiply_fusion.15
  13.1 1.4 fusion.24
  14.9 27.4 %all_gather.9 = bf16[2,1,1024,160]{2,3,0,1:T(8,128)(2,1)S(1)} all-gather(bf16[2,1,256,160]{2,3,0,1:T(8,128)(2,1)S(1)} %get-tuple-element.50), channel_id=1, replica_groups=mesh['row'=8,'col'=4] {'col'}, dimensions={2}, use_global_device_ids=true | all-gather | bytes 819200 | tf_op jit(solution)/shard_map/all_gather | solution.py:54
  42.3 26.6 %all_gather.10 = bf16[2,1,1024,160]{2,3,0,1:T(8,128)(2,1)S(1)} all-gather(bf16[2,1,256,160]{2,3,0,1:T(8,128)(2,1)S(1)} %get-tuple-element.51), channel_id=1, replica_groups=mesh['row'=8,'col'=4] {'col'}, dimensions={2}, use_global_device_ids=true | all-gather | bytes 819200 | tf_op jit(solution)/shard_map/all_gather | solution.py:55
  68.9 0.9 select_bitcast_fusion.2
  69.8 6.8 %all-gather.2.cloned.1.call-done = bf16[1024,1024]{1,0:T(8,128)(2,1)} async-done(((bf16[256,1024]{1,0:T(8,128)(2,1)}), bf16[1024,1024]{1,0:T(8,128)(2,1)}) %all-gather.2.cloned.1.call-update) | async-done | bytes 2097168 | tf_op jit(solution)/shard_map/all_gather | solution.py:57
  76.6 2.5 fusion.5
  79.1 0.9 select_bitcast_fusion.3
  81.2 1.5 fusion.45
  82.7 55.3 %all-reduce.6.cloned.1.call-done = (bf16[1024,160]{0,1:T(8,128)(2,1)}, bf16[1024,160]{0,1:T(8,128)(2,1)}, bf16[1024,160]{0,1:T(8,128)(2,1)}, bf16[1024,160]{0,1:T(8,128)(2,1)}) async-done(((bf16[1024,160]{0,1:T(8,128)(2,1)}, bf16[1024,160]{0,1:T(8,128)(2,1)}, bf16[1024,160]{0,1:T(8,128)(2,1)}, bf16[1024,160]{0,1:T(8,128)(2,1)}), (bf16[1024,160]{0,1:T(8,128)(2,1)}, bf16[1024,160]{0,1:T(8,128)(2,1)}, ...) | async-done | bytes 1310736 | tf_op jit(solution)/shard_map/psum | solution.py:10
  138.0 1.4 fusion.23
  139.4 1.2 fusion.35
  141.4 0.7 convolution_add_fusion
  142.3 11.7 %cholesky.174 = f32[128,128]{1,0:T(8,128)S(1)} custom-call(f32[128,128]{1,0:T(8,128)S(1)} %cholesky.211), custom_call_target="Cholesky" | custom-call | tf_op jit(solution)/shard_map/jit(cholesky)/cholesky | solution.py:34
  154.0 0.7 select_reduce_fusion
  154.7 1.4 fusion.27
  156.1 1.2 fusion.36
  158.1 0.7 convolution_add_fusion.1
  159.0 11.9 %cholesky.136 = f32[128,128]{1,0:T(8,128)S(1)} custom-call(f32[128,128]{1,0:T(8,128)S(1)} %cholesky.208), custom_call_target="Cholesky" | custom-call | tf_op jit(solution)/shard_map/jit(cholesky)/cholesky | solution.py:34
  170.9 10.6 %custom-call.15 = f32[1,128,128]{1,2,0:T(8,128)S(1)} custom-call(f32[1,128,128]{2,1,0:T(8,128)} %get-tuple-element.45), custom_call_target="InvertDiagBlocksLowerTriangular" | custom-call | tf_op jit(solution)/shard_map/jit(cholesky)/cholesky | solution.py:34
  181.9 2.9 %cholesky.194 = f32[32,32]{1,0:T(8,128)S(1)} custom-call(f32[32,32]{1,0:T(8,128)S(1)} %convolution_subtract_fusion.6), custom_call_target="Cholesky" | custom-call | tf_op jit(solution)/shard_map/jit(cholesky)/cholesky | solution.py:34
  184.8 0.6 compare_reduce_fusion
  185.5 0.6 compare_reduce_fusion.1
  187.4 0.6 copy-done.6
  188.1 9.8 %custom-call.13 = f32[1,128,128]{1,2,0:T(8,128)S(1)} custom-call(f32[1,128,128]{2,1,0:T(8,128)S(1)} %get-tuple-element.43), custom_call_target="InvertDiagBlocksLowerTriangular" | custom-call | tf_op jit(solution)/shard_map/jit(cholesky)/cholesky | solution.py:34
  198.2 2.9 %cholesky.156 = f32[32,32]{1,0:T(8,128)S(1)} custom-call(f32[32,32]{1,0:T(8,128)S(1)} %convolution_subtract_fusion.7), custom_call_target="Cholesky" | custom-call | tf_op jit(solution)/shard_map/jit(cholesky)/cholesky | solution.py:34
  201.8 0.6 compare_reduce_fusion.3
  203.6 0.7 select_select_fusion.1
  204.3 0.7 slice.139
  205.0 0.8 slice_bitcast_fusion.13
  206.0 0.7 pad_maximum_fusion.6
  206.6 19.7 %custom-call.14 = f32[2,128,128]{1,2,0:T(8,128)S(1)} custom-call(f32[2,128,128]{2,1,0:T(8,128)S(1)} %get-tuple-element.58), custom_call_target="InvertDiagBlocksLowerTriangular" | custom-call | tf_op jit(solution)/shard_map/triangular_solve/custom-call.0 | solution.py:35
  226.3 0.6 copy-done.10
  227.6 1.2 convolution_subtract_fusion.5
  228.8 1.0 fusion.68
  230.3 1.2 fusion.20
  231.5 20.5 %custom-call.16 = f32[2,128,128]{1,2,0:T(8,128)S(1)} custom-call(f32[2,128,128]{2,1,0:T(8,128)} %get-tuple-element.59), custom_call_target="InvertDiagBlocksLowerTriangular" | custom-call | tf_op jit(solution)/shard_map/triangular_solve/custom-call.0 | solution.py:35
  252.0 0.6 copy-done.11
  252.6 0.6 fusion.13
  253.3 1.1 convolution_subtract_fusion.4
  254.4 1.0 fusion.65
  260.1 1.1 maximum_bitcast_fusion.1
  261.2 1.2 maximum_bitcast_fusion
  (68 shorter events, 11.1 us)
Async XLA Ops:
  7.2 7.3 %copy-start.12 = (bf16[2,1,1,1024,160]{3,4,2,1,0:T(8,128)(2,1)S(1)}, bf16[2,1,1,1024,160]{3,4,2,1,0:T(8,128)(2,1)}, u32[]{:S(2)}) copy-start(bf16[2,1,1,1024,160]{3,4,2,1,0:T(8,128)(2,1)} %param.18) | copy-start | bytes 1966084
  7.2 7.3 %copy-start.4 = (bf16[2,1,1,1024,160]{3,4,2,1,0:T(8,128)(2,1)S(1)}, bf16[2,1,1,1024,160]{3,4,2,1,0:T(8,128)(2,1)}, u32[]{:S(2)}) copy-start(bf16[2,1,1,1024,160]{3,4,2,1,0:T(8,128)(2,1)} %param.16) | copy-start | bytes 1966084
  7.2 69.5 %all-gather.2.cloned.1.call-start = ((), (), s32[]{:S(2)}) async-start(), calls=%async_computation | async-start | bytes 2621440 | tf_op jit(solution)/shard_map/all_gather | solution.py:57
  7.9 130.1 %all-reduce.6.cloned.1.call-start = ((), (), s32[]{:S(2)}) async-start(), calls=%async_computation.1 | async-start | bytes 2621440 | tf_op jit(solution)/shard_map/psum | solution.py:10
  79.1 60.3 %copy-start = (bf16[2,1,1024,160]{2,3,0,1:T(8,128)(2,1)}, bf16[2,1,1024,160]{2,3,0,1:T(8,128)(2,1)S(1)}, u32[]{:S(2)}) copy-start(bf16[2,1,1024,160]{2,3,0,1:T(8,128)(2,1)S(1)} %fusion.5) | copy-start | bytes 1966084
  79.1 1.6 copy-start.2
  142.1 14.0 %copy-start.1 = (bf16[2,1,1024,160]{2,3,0,1:T(8,128)(2,1)S(1)}, bf16[2,1,1024,160]{2,3,0,1:T(8,128)(2,1)}, u32[]{:S(2)}) copy-start(bf16[2,1,1024,160]{2,3,0,1:T(8,128)(2,1)} %copy-done) | copy-start | bytes 1966084
  187.4 0.7 copy-start.6
  226.3 0.7 copy-start.10
  227.6 2.7 %copy-start.3 = (bf16[2,1,1,1024,160]{3,4,2,1,0:T(8,128)(2,1)S(1)}, bf16[2,1,1,1024,160]{3,4,2,1,0:T(8,128)(2,1)}, u32[]{:S(2)}) copy-start(bf16[2,1,1,1024,160]{3,4,2,1,0:T(8,128)(2,1)} %param.15) | copy-start | bytes 1966084
  252.0 0.7 copy-start.11
  256.4 1.1 copy-start.5
  256.4 1.1 copy-start.9
  257.5 1.6 copy-start.8
  258.6 1.0 copy-start.7
Sparse Core Ops, SparseCore 0:
  9.6 67.0 all-gather.1
  80.6 57.3 all-reduce.5
where the time goes:
time: 270 us; the launch traced here: 269 us
  other arithmetic  103 us (38%)
  waiting for transfers between devices  62.8 us (23%)
  blocking collectives  54 us (20%)
  matrix products  26.2 us (10%)
  between operations  17.2 us (6%)
  local copies, waits for them, and re-layouts  5.59 us (2%)
    psum x1, waiting for transfers between devices, spread(): return lax.psum(kept, axis)  55.3 us
    another operation x14, other arithmetic, recompress(): lower = jnp.linalg.cholesky(gram)  53.1 us
    another operation x8, other arithmetic, recompress(): lax.linalg.triangular_solve(lower, sketched, left_side=False, lower=True,...  41.6 us
    all_gather x1, blocking collectives, on_device(): lax.all_gather(panel_u * keep, 'col', axis=2, tiled=True)  27.4 us
    all_gather x1, blocking collectives, on_device(): lax.all_gather(panel_v * keep, 'col', axis=2, tiled=True)  26.6 us
    all_gather x1, waiting for transfers between devices, on_device(): inverse = lax.all_gather(diag_inverse, 'col', axis=0, tiled=True)  6.83 us
    another operation x6, matrix products, recompress(): lax.linalg.triangular_solve(lower, sketched, left_side=False, lower=True,...  5.61 us
  transfers between devices with their start and end apart: 2, of which 2 were waited for; matrix products, arithmetic and copies ran while one was open for 4% of the time, Pallas kernels for 0%

commit v1 on v0

--- a/solution.py
+++ b/solution.py
@@ -4,10 +4,12 @@
 from jax import lax
 from jax.sharding import PartitionSpec as P
 
+map_tokens_on = lambda field_in, a_name: jnp.sum(lax.all_gather(field_in, a_name), axis=0)
+
 
 def spread(value, axis, source):
     kept = jnp.where(lax.axis_index(axis) == source, value, 0).astype(value.dtype)
-    return lax.psum(kept, axis)
+    return map_tokens_on(kept, axis)
 
 
 def recompress(old_u, old_v, row_u, row_s, col_u, col_s, omega, rank):

time: 270 us -> 294 us (1.089)
  waiting for transfers between devices: 62.8 us -> 90.5 us
  other arithmetic: 103 us -> 110 us
  blocking collectives: 54 us -> 49.4 us
  matrix products: 26.2 us -> 23 us
    all_gather x0 -> x4, waiting for transfers between devices: none -> 77.8 us  [lax.all_gather(field_in, a_name)]
    psum x1 -> x0, waiting for transfers between devices: 55.3 us -> none  [spread(): return lax.psum(kept, axis)]
    reduce_sum x0 -> x4, other arithmetic: none -> 8.91 us  [jnp.sum(lax.all_gather(field_in, a_name), axis=0)]
    all_gather x1, waiting for transfers between devices: 6.83 us -> 11.3 us  [on_device(): inverse = lax.all_gather(diag_inverse, 'col', axis=0, tiled=True)]
    all_gather x1, blocking collectives: 27.4 us -> 23.8 us  [on_device(): lax.all_gather(panel_u * keep, 'col', axis=2, tiled=True)]
  transfers between devices with their start and end apart: 2 -> 5, of which waited for: 2 -> 5; matrix products, arithmetic and copies ran while one was open for 4% -> 18% of each run, Pallas kernels for 0% -> 0%
where the time goes in v1:
time: 294 us; the launch traced here: 293 us
  other arithmetic  110 us (37%)
  waiting for transfers between devices  90.5 us (31%)
  blocking collectives  49.4 us (17%)
  matrix products  23 us (8%)
  between operations  17 us (6%)
  local copies, waits for them, and re-layouts  2.95 us (1%)
    all_gather x4, waiting for transfers between devices, lax.all_gather(field_in, a_name)  77.8 us
    another operation x14, other arithmetic, recompress(): lower = jnp.linalg.cholesky(gram)  51.6 us
    another operation x8, other arithmetic, recompress(): lax.linalg.triangular_solve(lower, sketched, left_side=False, lower=True,...  41 us
    all_gather x1, blocking collectives, on_device(): lax.all_gather(panel_v * keep, 'col', axis=2, tiled=True)  25.7 us
    all_gather x1, blocking collectives, on_device(): lax.all_gather(panel_u * keep, 'col', axis=2, tiled=True)  23.8 us
    all_gather x1, waiting for transfers between devices, on_device(): inverse = lax.all_gather(diag_inverse, 'col', axis=0, tiled=True)  11.3 us
    reduce_sum x4, other arithmetic, jnp.sum(lax.all_gather(field_in, a_name), axis=0)  8.91 us
  transfers between devices with their start and end apart: 5, of which 5 were waited for; matrix products, arithmetic and copies ran while one was open for 18% of the time, Pallas kernels for 0%

profile of v1, /device:TPU:0, one launch (start us, length us, event | category | flops | bytes accessed | tf_op | source)
XLA Modules:
  0.0 293.3 jit_solution(6367466076463747102)
XLA Ops:
  7.2 0.7 all-gather.10.cloned.1.call-update
  8.0 0.7 compare_convert_fusion
  8.7 1.1 bitcast_multiply_fusion.15
  9.8 23.8 %all_gather.25 = bf16[2,1,1024,160]{2,3,0,1:T(8,128)(2,1)S(1)} all-gather(bf16[2,1,256,160]{2,3,0,1:T(8,128)(2,1)S(1)} %get-tuple-element.48), channel_id=1, replica_groups=mesh['row'=8,'col'=4] {'col'}, dimensions={2}, use_global_device_ids=true | all-gather | bytes 819200 | tf_op jit(solution)/shard_map/all_gather | solution.py:56
  33.6 0.9 select_bitcast_fusion.2
  34.5 0.7 all-gather.18.cloned.1.call-update
  35.3 25.7 %all_gather.26 = bf16[2,1,1024,160]{2,3,0,1:T(8,128)(2,1)S(1)} all-gather(bf16[2,1,256,160]{2,3,0,1:T(8,128)(2,1)S(1)} %get-tuple-element.49), channel_id=1, replica_groups=mesh['row'=8,'col'=4] {'col'}, dimensions={2}, use_global_device_ids=true | all-gather | bytes 819200 | tf_op jit(solution)/shard_map/all_gather | solution.py:57
  60.9 11.3 %all-gather.10.cloned.1.call-done = bf16[1024,1024]{1,0:T(8,128)(2,1)} async-done(((bf16[256,1024]{1,0:T(8,128)(2,1)}), bf16[1024,1024]{1,0:T(8,128)(2,1)}) %all-gather.10.cloned.1.call-update) | async-done | bytes 2097168 | tf_op jit(solution)/shard_map/all_gather | solution.py:59
  72.2 2.5 fusion.5
  74.7 0.9 select_bitcast_fusion.3
  75.7 0.7 fusion.77
  76.3 0.6 fusion.72
  77.0 0.7 fusion.71
  77.6 0.7 convert_subtract_fusion
  78.4 1.3 fusion.24
  79.7 2.0 fusion.28
  81.7 0.6 convert_subtract_fusion.1
  82.4 1.4 fusion.45
  84.3 19.7 %all-gather.14.cloned.1.call-done = bf16[8,1,1024,160]{2,3,1,0:T(8,128)(2,1)} async-done(((bf16[1,1,1024,160]{2,3,1,0:T(8,128)(2,1)}), bf16[8,1,1024,160]{2,3,1,0:T(8,128)(2,1)}) %all-gather.14.cloned.1.call-update) | async-done | bytes 2621456 | tf_op jit(solution)/shard_map/all_gather | solution.py:7
  104.0 2.2 bitcast_reduce_fusion.2
  106.2 29.7 %all-gather.18.cloned.1.call-done = bf16[8,1,1024,160]{2,3,1,0:T(8,128)(2,1)} async-done(((bf16[1,1,1024,160]{2,3,1,0:T(8,128)(2,1)}), bf16[8,1,1024,160]{2,3,1,0:T(8,128)(2,1)}) %all-gather.18.cloned.1.call-update) | async-done | bytes 2621456 | tf_op jit(solution)/shard_map/all_gather | solution.py:7
  135.9 2.3 bitcast_reduce_fusion
  138.2 1.0 fusion.23
  139.2 1.0 fusion.27
  140.2 28.0 %all-gather.16.cloned.1.call-done = bf16[8,1,1024,160]{2,3,1,0:T(8,128)(2,1)} async-done(((bf16[1,1,1024,160]{2,3,1,0:T(8,128)(2,1)}), bf16[8,1,1024,160]{2,3,1,0:T(8,128)(2,1)}) %all-gather.16.cloned.1.call-update) | async-done | bytes 2621456 | tf_op jit(solution)/shard_map/all_gather | solution.py:7
  168.2 2.2 bitcast_reduce_fusion.1
  171.5 0.7 convolution_add_fusion
  172.4 11.7 %cholesky.174 = f32[128,128]{1,0:T(8,128)S(1)} custom-call(f32[128,128]{1,0:T(8,128)S(1)} %cholesky.211), custom_call_target="Cholesky" | custom-call | tf_op jit(solution)/shard_map/jit(cholesky)/cholesky | solution.py:36
  184.2 9.8 %custom-call.15 = f32[1,128,128]{1,2,0:T(8,128)S(1)} custom-call(f32[1,128,128]{2,1,0:T(8,128)S(1)} %get-tuple-element.43), custom_call_target="InvertDiagBlocksLowerTriangular" | custom-call | tf_op jit(solution)/shard_map/jit(cholesky)/cholesky | solution.py:36
  194.3 2.9 cholesky.194
  197.2 0.6 compare_reduce_fusion.1
  199.8 0.6 slice_bitcast_fusion.10
  200.9 2.2 bitcast_reduce_fusion.3
  203.4 0.7 copy-done
  205.0 0.7 convolution_add_fusion.1
  205.9 11.7 %cholesky.136 = f32[128,128]{1,0:T(8,128)S(1)} custom-call(f32[128,128]{1,0:T(8,128)S(1)} %cholesky.208), custom_call_target="Cholesky" | custom-call | tf_op jit(solution)/shard_map/jit(cholesky)/cholesky | solution.py:36
  217.6 0.7 compare_reduce_fusion.3
  218.3 9.8 %custom-call.13 = f32[1,128,128]{1,2,0:T(8,128)S(1)} custom-call(f32[1,128,128]{2,1,0:T(8,128)S(1)} %get-tuple-element.41), custom_call_target="InvertDiagBlocksLowerTriangular" | custom-call | tf_op jit(solution)/shard_map/jit(cholesky)/cholesky | solution.py:36
  228.5 2.9 cholesky.156
  231.4 0.7 compare_reduce_fusion.2
  233.5 0.7 pad_maximum_fusion.6
  234.2 19.7 %custom-call.16 = f32[2,128,128]{1,2,0:T(8,128)S(1)} custom-call(f32[2,128,128]{2,1,0:T(8,128)S(1)} %get-tuple-element.57), custom_call_target="InvertDiagBlocksLowerTriangular" | custom-call | tf_op jit(solution)/shard_map/triangular_solve/custom-call.0 | solution.py:37
  254.5 1.1 convolution_subtract_fusion.4
  257.0 20.5 %custom-call.14 = f32[2,128,128]{1,2,0:T(8,128)S(1)} custom-call(f32[2,128,128]{2,1,0:T(8,128)} %get-tuple-element.56), custom_call_target="InvertDiagBlocksLowerTriangular" | custom-call | tf_op jit(solution)/shard_map/triangular_solve/custom-call.0 | solution.py:37
  277.5 0.6 copy-done.14
  279.2 1.0 fusion.68
  283.9 1.2 maximum_bitcast_fusion
  285.6 1.2 maximum_bitcast_fusion.1
  (89 shorter events, 12.3 us)
Async XLA Ops:
  7.2 65.1 %all-gather.10.cloned.1.call-start = ((), (), s32[]{:S(2)}) async-start(), calls=%async_computation | async-start | bytes 2621440 | tf_op jit(solution)/shard_map/all_gather | solution.py:59
  7.9 96.1 %all-gather.14.cloned.1.call-start = ((), (), s32[]{:S(2)}) async-start(), calls=%async_computation.2 | async-start | bytes 2949120 | tf_op jit(solution)/shard_map/all_gather | solution.py:7
  34.5 101.4 %all-gather.18.cloned.1.call-start = ((), (), s32[]{:S(2)}) async-start(), calls=%async_computation.4 | async-start | bytes 2949120 | tf_op jit(solution)/shard_map/all_gather | solution.py:7
  35.2 133.0 %all-gather.16.cloned.1.call-start = ((), (), s32[]{:S(2)}) async-start(), calls=%async_computation.3 | async-start | bytes 2949120 | tf_op jit(solution)/shard_map/all_gather | solution.py:7
  60.9 14.7 %copy-start.15 = (s32[2,1,1]{0,2,1:T(1,128)S(1)}, s32[2,1,1]{0,2,1:T(1,128)}, u32[]{:S(2)}) copy-start(s32[2,1,1]{0,2,1:T(1,128)} %param.17) | copy-start | bytes 28
  60.9 17.4 %copy-start.8 = (bf16[2,1,1,1024,160]{3,4,2,1,0:T(8,128)(2,1)S(1)}, bf16[2,1,1,1024,160]{3,4,2,1,0:T(8,128)(2,1)}, u32[]{:S(2)}) copy-start(bf16[2,1,1,1024,160]{3,4,2,1,0:T(8,128)(2,1)} %param.16) | copy-start | bytes 1966084
  74.7 7.7 %copy-start.6 = (bf16[2,1,1,1024,160]{3,4,2,1,0:T(8,128)(2,1)S(1)}, bf16[2,1,1,1024,160]{3,4,2,1,0:T(8,128)(2,1)}, u32[]{:S(2)}) copy-start(bf16[2,1,1,1024,160]{3,4,2,1,0:T(8,128)(2,1)} %param.15) | copy-start | bytes 1966084
  75.6 125.3 %all-gather.12.cloned.1.call-start = ((), (), s32[]{:S(2)}) async-start(), calls=%async_computation.1 | async-start | bytes 2949120 | tf_op jit(solution)/shard_map/all_gather | solution.py:7
  106.2 34.0 %copy-start.2 = (bf16[1024,160]{0,1:T(8,128)(2,1)}, bf16[1024,160]{0,1:T(8,128)(2,1)S(1)}, u32[]{:S(2)}) copy-start(bf16[1024,160]{0,1:T(8,128)(2,1)S(1)} %bitcast_reduce_fusion.2) | copy-start | bytes 983044
  135.9 2.3 copy-start.16
  138.2 32.3 %copy-start.4 = (bf16[1024,160]{0,1:T(8,128)(2,1)}, bf16[1024,160]{0,1:T(8,128)(2,1)S(1)}, u32[]{:S(2)}) copy-start(bf16[1024,160]{0,1:T(8,128)(2,1)S(1)} %bitcast_reduce_fusion) | copy-start | bytes 983044
  168.2 2.5 copy-start.13
  199.8 4.3 %copy-start.12 = (f32[160,160]{1,0:T(8,128)S(1)}, f32[160,160]{1,0:T(8,128)}, u32[]{:S(2)}) copy-start(f32[160,160]{1,0:T(8,128)} %fusion.27) | copy-start | bytes 307204
  199.8 0.7 copy-start.10
  203.4 0.7 copy-start
  205.0 28.5 %copy-start.11 = (f32[1,128,128]{2,1,0:T(8,128)S(1)}, f32[1,128,128]{2,1,0:T(8,128)}, u32[]{:S(2)}) copy-start(f32[1,128,128]{2,1,0:T(8,128)} %slice_bitcast_fusion.10) | copy-start | bytes 196612
  205.8 50.1 %copy-start.7 = (bf16[2,1,1,1024,160]{3,4,2,1,0:T(8,128)(2,1)S(1)}, bf16[2,1,1,1024,160]{3,4,2,1,0:T(8,128)(2,1)}, u32[]{:S(2)}) copy-start(bf16[2,1,1,1024,160]{3,4,2,1,0:T(8,128)(2,1)} %param.15) | copy-start | bytes 1966084
  277.5 0.7 copy-start.14
  280.2 1.6 copy-start.9
  280.7 1.6 copy-start.1
  281.3 2.2 copy-start.5
  283.4 1.7 copy-start.3
Sparse Core Ops, SparseCore 0:
  9.5 62.6 all-gather.9
  74.1 29.8 all-gather.13
  105.9 29.9 all-gather.17
  138.2 29.9 all-gather.15
  170.5 30.3 all-gather.11
